TPU v7x, 128 devices: a whole 4x4x4 slice. The times are simulated.
128 devices in a mesh: side: 2 (over y_hi), dev: 64 (over y_lo, z, x, core).
Axes of the slice: x: 4, y: 4 (y_hi: 2, y_lo: 2; y = y_hi * 2 + y_lo), z: 4, core: 2. Of those that a mesh axis runs over, the one named last changes fastest.
Arguments:
- queries: bfloat16 [2048, 8192], P('dev', 'side'), may hold values from -6 to 6
- cache_keys: bfloat16 [2048, 256, 512], P('dev', None, 'side'), may hold values from -6 to 6
- cache_values: bfloat16 [2048, 256, 512], P('dev', None, 'side'), may hold values from -6 to 6
- new_key: bfloat16 [2048, 512], P('dev', 'side'), may hold values from -15 to 15
- new_value: bfloat16 [2048, 512], P('dev', 'side'), may hold values from -6 to 6
- cache_lengths: int32 [2048], P('dev'), may hold values from 2 to 256, as said below
- hidden: bfloat16 [2048, 4096], P('dev'), may hold values from -6 to 6
- norm_gain: bfloat16 [4096], replicated, may hold values from 0.099609375 to 1.8984375
- expert_ids: int32 [2048, 8], P('dev'), may hold values from 0 to 63, all different within a row; in each aligned block of 32 rows (0 to 31, 32 to 63, ...) at most 8 rows name the same one
- router_probs: float32 [2048, 8], P('dev'), may hold values from 0.02 to 1
- w_gate: bfloat16 [64, 4096, 1536], P('dev', None, 'side'), may hold values from -0.09375 to 0.09375
- w_up: bfloat16 [64, 4096, 1536], P('dev', None, 'side'), may hold values from -0.09375 to 0.09375
- w_down: bfloat16 [64, 1536, 4096], P('dev', 'side'), may hold values from -0.15625 to 0.15625
Outputs:
- context: bfloat16 [2048, 8192], P('dev', 'side')
- moe_out: bfloat16 [2048, 4096], P('dev')
Inputs may be any that keep to these rules, and one draw needn't show every extreme that they name: `expert_ids`: in each aligned block of 32 rows (the rows of one dev index) no expert is named more than 8 times, a bound that some block reaches. `cache_lengths`: every aligned block of 32 tokens holds a token with 256 valid positions.
All inputs are finite; a program needn't handle non-finite values.
Results may differ from a plain program's by a relative error of at most 0.012.
Values may be sent and summed in bfloat16 or wider, within the bound.
A program may use at most 128 MiB of HBM per device.

v0:
```python
import jax
import jax.numpy as jnp
from jax import lax
from jax.sharding import PartitionSpec as P

HEADS = 64
KV_HEADS = 4
HEAD_DIM = 128


def route_onehot(block_ids, expert_count, capacity):
    flat_ids = block_ids.reshape(-1)
    expert_hot = (flat_ids[:, None] == jnp.arange(expert_count, dtype=jnp.int32)[None, :]).astype(
        jnp.int32
    )
    earlier = jnp.cumsum(expert_hot, axis=0) - expert_hot
    slot_rank = jnp.sum(earlier * expert_hot, axis=1)
    slot_hot = (slot_rank[:, None] == jnp.arange(capacity, dtype=jnp.int32)[None, :]).astype(
        jnp.float32
    )
    route_hot = expert_hot.astype(jnp.float32)[:, :, None] * slot_hot[:, None, :]
    return route_hot.reshape(block_ids.shape[0], block_ids.shape[1], expert_count, capacity)


def attend_local(queries, cache_keys, cache_values, new_key, new_value, cache_lengths):
    row_count = queries.shape[0]
    cache_len = cache_keys.shape[1]
    groups = cache_keys.shape[2] // HEAD_DIM
    per_group = HEADS // KV_HEADS
    score_scale = HEAD_DIM ** (-0.5)
    query_heads = queries.reshape(row_count, groups, per_group, HEAD_DIM)
    key_heads = cache_keys.reshape(row_count, cache_len, groups, HEAD_DIM)
    value_heads = cache_values.reshape(row_count, cache_len, groups, HEAD_DIM)
    scores = (
        jnp.einsum("tgqd,tlgd->tgql", query_heads, key_heads, preferred_element_type=jnp.float32)
        * score_scale
    )
    own_key = new_key.reshape(row_count, groups, HEAD_DIM)
    own_score = (
        jnp.einsum("tgqd,tgd->tgq", query_heads, own_key, preferred_element_type=jnp.float32)
        * score_scale
    )
    visible = jnp.arange(cache_len, dtype=jnp.int32)[None, :] < cache_lengths[:, None]
    scores = jnp.where(visible[:, None, None, :], scores, -1e30)
    top_score = jnp.maximum(jnp.max(scores, axis=3), own_score)
    exp_scores = jnp.exp(scores - top_score[..., None])
    own_exp = jnp.exp(own_score - top_score)
    denominator = jnp.sum(exp_scores, axis=3) + own_exp
    attn_weights = (exp_scores / denominator[..., None]).astype(jnp.bfloat16)
    own_prob = (own_exp / denominator).astype(jnp.bfloat16)
    combined = jnp.einsum(
        "tgql,tlgd->tgqd", attn_weights, value_heads, preferred_element_type=jnp.float32
    )
    own_value = new_value.reshape(row_count, groups, 1, HEAD_DIM).astype(jnp.float32)
    combined = combined + own_prob.astype(jnp.float32)[..., None] * own_value
    return combined.reshape(row_count, groups * per_group * HEAD_DIM).astype(jnp.bfloat16)


def per_device(
    queries,
    cache_keys,
    cache_values,
    new_key,
    new_value,
    cache_lengths,
    hidden,
    norm_gain,
    expert_ids,
    router_probs,
    w_gate,
    w_up,
    w_down,
):
    context = attend_local(queries, cache_keys, cache_values, new_key, new_value, cache_lengths)
    row_count = hidden.shape[0]
    top_count = expert_ids.shape[1]
    devices = lax.axis_size("dev")
    experts = w_gate.shape[0] * devices
    capacity = max(2, 2 * row_count * top_count // experts)
    gate_share = router_probs / jnp.sum(router_probs, axis=1, keepdims=True)
    hidden_wide = hidden.astype(jnp.float32)
    inverse = lax.rsqrt(jnp.mean(hidden_wide * hidden_wide, axis=1, keepdims=True) + 1e-06)
    normed = (hidden_wide * inverse * norm_gain.astype(jnp.float32)[None, :]).astype(jnp.bfloat16)
    route_hot = route_onehot(expert_ids, experts, capacity)
    slot_hot = jnp.sum(route_hot, axis=1)
    slot_gate = jnp.sum(route_hot * gate_share[:, :, None, None], axis=1)
    buffer = jnp.einsum(
        "rec,rd->ecd", slot_hot.astype(jnp.bfloat16), normed, preferred_element_type=jnp.float32
    ).astype(jnp.bfloat16)
    row_block = lax.all_to_all(buffer, "dev", split_axis=0, concat_axis=0, tiled=True)
    gate_act = jnp.einsum("scd,df->scf", row_block, w_gate[0], preferred_element_type=jnp.float32)
    up_act = jnp.einsum("scd,df->scf", row_block, w_up[0], preferred_element_type=jnp.float32)
    activation = (jax.nn.silu(gate_act) * up_act).astype(jnp.bfloat16)
    partial_out = jnp.einsum(
        "scf,fd->scd", activation, w_down[0], preferred_element_type=jnp.float32
    ).astype(jnp.bfloat16)
    back = lax.all_to_all(partial_out, "dev", split_axis=0, concat_axis=0, tiled=True)
    local_mix = jnp.einsum(
        "rec,ecd->rd", slot_gate, back.astype(jnp.float32), precision=lax.Precision.HIGHEST
    )
    combined = lax.psum(local_mix, "side")
    return (context, combined.astype(jnp.bfloat16))


def solution(mesh):
    in_specs = (
        P("dev", "side"),
        P("dev", None, "side"),
        P("dev", None, "side"),
        P("dev", "side"),
        P("dev", "side"),
        P("dev"),
        P("dev", None),
        P(),
        P("dev", None),
        P("dev", None),
        P("dev", None, "side"),
        P("dev", None, "side"),
        P("dev", "side", None),
    )
    out_specs = (P("dev", "side"), P("dev", None))
    return jax.shard_map(
        per_device, mesh=mesh, in_specs=in_specs, out_specs=out_specs, check_vma=False
    )
```

profile of v0, /device:TPU:2, one launch (start us, length us, event | category | flops | bytes accessed | tf_op | source)
XLA Modules:
  0.0 173.4 jit_solution(5468898151774488935)
XLA Ops:
  0.6 0.8 copy.38
  1.7 0.6 reduce-window.6
  2.3 0.2 slice_reduce_fusion
  2.9 0.7 reduce_sum.56
  3.6 0.7 broadcast_divide_fusion
  4.3 0.7 multiply_reduce_fusion
  5.2 0.7 convert_element_type.92
  5.9 1.1 fusion.32
  7.0 2.4 %convolution_convert_fusion = bf16[64,8,4096]{2,1,0:T(8,128)(2,1)S(1)} fusion(bf16[32,64,8]{0,2,1:T(8,128)(2,1)S(1)} %copy.43, bf16[32,4096]{1,0:T(8,128)(2,1)} %param.19, f32[4096]{0:T(1024)S(1)} %convert_element_type.92, f32[32]{0:T(128)S(1)} %add_rsqrt_fusion), kind=kOutput, calls=%fused_computation.7 | convolution fusion | flops 136839168 | bytes 4505728 | tf_op jit(solution)/shard_map/rec,rd->ecd/dot_general | solution.py:87
  9.5 61.6 %all_to_all.10 = bf16[64,8,4096]{2,1,0:T(8,128)(2,1)S(1)} all-to-all(bf16[64,8,4096]{2,1,0:T(8,128)(2,1)S(1)} %convolution_convert_fusion), channel_id=1, replica_groups=mesh['side'=2,'dev'=64] {'dev'}, dimensions={0} | all-to-all | bytes 8388608 | tf_op jit(solution)/shard_map/all_to_all | solution.py:90
  71.1 3.5 %fusion.4 = f32[64,8,768]{2,1,0:T(8,128)S(1)} fusion(bf16[64,8,4096]{2,1,0:T(8,128)(2,1)S(1)} %all_to_all.10, bf16[1,4096,768]{2,1,0:T(8,128)(2,1)S(1)} %bitcast.90), kind=kOutput, calls=%fused_computation.4 | convolution fusion | flops 3221225472 | bytes 12058624 | tf_op jit(solution)/shard_map/scd,df->scf/dot_general | solution.py:91
  74.6 3.6 %multiply_convert_fusion = bf16[64,8,768]{2,1,0:T(8,128)(2,1)S(1)} fusion(f32[64,8,768]{2,1,0:T(8,128)S(1)} %fusion.4, bf16[64,8,4096]{2,1,0:T(8,128)(2,1)S(1)} %all_to_all.10, bf16[1,4096,768]{2,1,0:T(8,128)(2,1)S(1)} %bitcast.92), kind=kOutput, calls=%fused_computation.15 | convolution fusion | flops 3223584768 | bytes 12845056 | tf_op jit(solution)/shard_map/scd,df->scf/dot_general | solution.py:92
  78.2 3.7 %fusion.6 = bf16[64,8,4096]{2,0,1:T(8,128)(2,1)S(1)} fusion(bf16[1,768,4096]{2,1,0:T(8,128)(2,1)S(1)} %bitcast.94, bf16[64,8,768]{2,1,0:T(8,128)(2,1)S(1)} %multiply_convert_fusion), kind=kOutput, calls=%fused_computation.6 | convolution fusion | flops 3223322624 | bytes 11272192 | tf_op jit(solution)/shard_map/scf,fd->scd/dot_general | solution.py:94
  81.9 4.3 %copy.45 = bf16[64,8,4096]{2,1,0:T(8,128)(2,1)} copy(bf16[64,8,4096]{2,0,1:T(8,128)(2,1)S(1)} %fusion.6) | data formatting | bytes 8388608 | tf_op jit(solution)/shard_map/convert_element_type | solution.py:96
  86.2 5.7 %all-to-all-start.1 = ((bf16[64,8,4096]{2,1,0:T(8,128)(2,1)}), bf16[64,8,4096]{2,1,0:T(8,128)(2,1)}, u32[]{:S(2)}, u32[]{:S(2)}) async-start(bf16[64,8,4096]{2,1,0:T(8,128)(2,1)} %copy.45), calls=%async_computation.1 | async-start | bytes 8388608 | tf_op jit(solution)/shard_map/all_to_all | solution.py:97
  92.1 0.2 fusion.49
  92.3 3.7 %fusion.48 = (f32[32,2,16]{2,1,0:T(2,128)S(1)}, f32[32,2,16,256]{3,2,1,0:T(8,128)S(1)}) fusion(bf16[32,2,16,128]{3,2,1,0:T(8,128)(2,1)S(1)} %bitcast.83, pred[32,256]{1,0:T(8,128)(4,1)S(1)} %iota_compare_fusion.4, bf16[32,256,256]{2,1,0:T(8,128)(2,1)} %param.14), kind=kOutput, calls=%fused_computation.59 | convolution fusion | flops 67894272 | bytes 5517312 | tf_op jit(solution)/shard_map/tgqd,tlgd->tgql/dot_general | solution.py:35
  96.0 0.4 fusion.30
  96.6 1.0 fusion.26
  97.6 0.8 copy.80
  98.4 0.2 copy.50
  98.6 47.8 %all-to-all-done.1 = bf16[64,8,4096]{2,1,0:T(8,128)(2,1)} async-done(((bf16[64,8,4096]{2,1,0:T(8,128)(2,1)}), bf16[64,8,4096]{2,1,0:T(8,128)(2,1)}, u32[]{:S(2)}, u32[]{:S(2)}) %all-to-all-start.1) | async-done | bytes 4194336 | tf_op jit(solution)/shard_map/all_to_all | solution.py:97
  146.4 4.4 %convolution_bitcast_fusion = f32[32,4096]{1,0:T(8,128)S(1)} fusion(f32[32,64,8]{0,2,1:T(8,128)S(1)} %copy.50, bf16[64,8,4096]{2,1,0:T(8,128)(2,1)} %all-to-all-done.1), kind=kOutput, calls=%fused_computation.8 | convolution fusion | flops 805306368 | bytes 4784128 | tf_op jit(solution)/shard_map/rec,ecd->rd/dot_general | solution.py:98
  150.8 22.6 %all-reduce.1 = bf16[32,4096]{1,0:T(8,128)(2,1)} all-reduce(f32[32,4096]{1,0:T(8,128)S(1)} %convolution_bitcast_fusion), channel_id=1, replica_groups=mesh['side'=2,'dev'=64] {'side'}, use_global_device_ids=true, to_apply=%region_9.10 | all-reduce | flops 131072 | bytes 786432 | tf_op jit(solution)/shard_map/psum | solution.py:101
  (43 shorter events, 1.2 us)
Async XLA Ops:
  7.0 64.1 %slice-start = ((s8[6291456]{0:T(1024)(128)(4,1)}), s8[4194304]{0:T(1024)(128)(4,1)S(1)}, s32[]{:S(2)}) async-start(s8[6291456]{0:T(1024)(128)(4,1)} %bitcast.89), calls=%async_computation.2 | async-start | bytes 8388608
  9.4 61.7 %slice-start.1 = ((s8[6291456]{0:T(1024)(128)(4,1)}), s8[2097152]{0:T(1024)(128)(4,1)S(1)}, s32[]{:S(2)}) async-start(s8[6291456]{0:T(1024)(128)(4,1)} %bitcast.89), calls=%async_computation.3 | async-start | bytes 4194304
  9.4 65.1 %slice-start.2 = ((s8[6291456]{0:T(1024)(128)(4,1)}), s8[4194304]{0:T(1024)(128)(4,1)S(1)}, s32[]{:S(2)}) async-start(s8[6291456]{0:T(1024)(128)(4,1)} %bitcast.91), calls=%async_computation.4 | async-start | bytes 8388608
  71.1 3.5 %slice-start.3 = ((s8[6291456]{0:T(1024)(128)(4,1)}), s8[2097152]{0:T(1024)(128)(4,1)S(1)}, s32[]{:S(2)}) async-start(s8[6291456]{0:T(1024)(128)(4,1)} %bitcast.91), calls=%async_computation.5 | async-start | bytes 4194304
  71.1 7.1 %slice-start.4 = ((s8[6291456]{0:T(1024)(128)(4,1)}), s8[4194304]{0:T(1024)(128)(4,1)S(1)}, s32[]{:S(2)}) async-start(s8[6291456]{0:T(1024)(128)(4,1)} %bitcast.93), calls=%async_computation.6 | async-start | bytes 8388608
  74.6 3.6 %slice-start.5 = ((s8[6291456]{0:T(1024)(128)(4,1)}), s8[2097152]{0:T(1024)(128)(4,1)S(1)}, s32[]{:S(2)}) async-start(s8[6291456]{0:T(1024)(128)(4,1)} %bitcast.93), calls=%async_computation.7 | async-start | bytes 4194304
  86.2 5.7 %copy-start = (bf16[32,4096]{1,0:T(8,128)(2,1)S(1)}, bf16[32,4096]{1,0:T(8,128)(2,1)}, u32[]{:S(2)}) copy-start(bf16[32,4096]{1,0:T(8,128)(2,1)} %param.13) | copy-start | bytes 786436
  86.2 5.8 %copy-start.1 = (bf16[32,256]{1,0:T(8,128)(2,1)S(1)}, bf16[32,256]{1,0:T(8,128)(2,1)}, u32[]{:S(2)}) copy-start(bf16[32,256]{1,0:T(8,128)(2,1)} %param.16) | copy-start | bytes 49156
  86.2 5.8 %copy-start.2 = (bf16[32,256]{1,0:T(8,128)(2,1)S(1)}, bf16[32,256]{1,0:T(8,128)(2,1)}, u32[]{:S(2)}) copy-start(bf16[32,256]{1,0:T(8,128)(2,1)} %param.17) | copy-start | bytes 49156
  86.2 5.8 %copy-start.3 = (s32[32]{0:T(128)S(1)}, s32[32]{0:T(128)}, u32[]{:S(2)}) copy-start(s32[32]{0:T(128)} %param.18) | copy-start | bytes 388
  86.2 60.2 %all-to-all-start.1 = ((bf16[64,8,4096]{2,1,0:T(8,128)(2,1)}), bf16[64,8,4096]{2,1,0:T(8,128)(2,1)}, u32[]{:S(2)}, u32[]{:S(2)}) async-start(bf16[64,8,4096]{2,1,0:T(8,128)(2,1)} %copy.45), calls=%async_computation.1 | async-start | bytes 8388608 | tf_op jit(solution)/shard_map/all_to_all | solution.py:97
  92.0 4.6 %copy-start.4 = (bf16[32,256,256]{2,1,0:T(8,128)(2,1)S(1)}, bf16[32,256,256]{2,1,0:T(8,128)(2,1)}, u32[]{:S(2)}) copy-start(bf16[32,256,256]{2,1,0:T(8,128)(2,1)} %param.15) | copy-start | bytes 12582916
where the time goes:
time: 174 us; the launch traced here: 173 us
  blocking collectives  84.2 us (48%)
  waiting for transfers between devices  47.8 us (27%)
  matrix products  22.4 us (13%)
  local copies, waits for them, and re-layouts  6.81 us (4%)
  starting transfers between devices  5.68 us (3%)
  other arithmetic  5.51 us (3%)
    all_to_all x1, blocking collectives, per_device(): lax.all_to_all(buffer, 'dev', split_axis=0, concat_axis=0, tiled=True)  61.6 us
    all_to_all x1, waiting for transfers between devices, per_device(): lax.all_to_all(partial_out, 'dev', split_axis=0, concat_axis=0, tiled=True)  47.8 us
    psum x1, blocking collectives, per_device(): combined = lax.psum(local_mix, 'side')  22.6 us
    all_to_all x1, starting transfers between devices, per_device(): lax.all_to_all(partial_out, 'dev', split_axis=0, concat_axis=0, tiled=True)  5.68 us
    dot_general x1, matrix products, per_device(): jnp.einsum('rec,ecd->rd', slot_gate, back.astype(jnp.float32), precision=...  4.42 us
    convert_element_type x1, local copies, waits for them, and re-layouts, per_device(): partial_out = jnp.einsum('scf,fd->scd', activation, w_down[0], preferred_...  4.27 us
    dot_general x1, matrix products, attend_local(): jnp.einsum('tgqd,tlgd->tgql', query_heads, key_heads, preferred_element_t...  3.67 us
    dot_general x1, matrix products, per_device(): jnp.einsum('scf,fd->scd', activation, w_down[0], preferred_element_type=j...  3.66 us
  transfers between devices with their start and end apart: 1, of which 1 were waited for; matrix products, arithmetic and copies ran while one was open for 4% of the time, Pallas kernels for 0%

commit v1 on v0

--- a/solution.py
+++ b/solution.py
@@ -98,7 +98,7 @@
     local_mix = jnp.einsum(
         "rec,ecd->rd", slot_gate, back.astype(jnp.float32), precision=lax.Precision.HIGHEST
     )
-    combined = lax.psum(local_mix, "side")
+    combined = jnp.sum(lax.all_gather(local_mix, "side"), axis=0)
     return (context, combined.astype(jnp.bfloat16))
 
 

time: 174 us -> 193 us (1.11)
  waiting for transfers between devices: 47.8 us -> 70.7 us
  blocking collectives: 84.2 us -> 61.6 us
  between operations: 0.93 us -> 14.3 us
  matrix products: 22.4 us -> 25 us
  other arithmetic: 5.51 us -> 7.59 us
    psum x1 -> x0, blocking collectives: 22.6 us -> none  [per_device(): combined = lax.psum(local_mix, 'side')]
    all_gather x0 -> x1, waiting for transfers between devices: none -> 20.6 us  [per_device(): combined = jnp.sum(lax.all_gather(local_mix, 'side'), axis=0)]
    all_to_all x1, waiting for transfers between devices: 47.8 us -> 50.1 us  [per_device(): lax.all_to_all(partial_out, 'dev', split_axis=0, concat_axis=0, tiled=True)]
    reduce_sum x0 -> x1, other arithmetic: none -> 2.07 us  [per_device(): combined = jnp.sum(lax.all_gather(local_mix, 'side'), axis=0)]
    dot_general x1, matrix products: 1 us -> 2.96 us  [attend_local(): jnp.einsum('tgql,tlgd->tgqd', attn_weights, value_heads, preferred_elemen...]
  transfers between devices with their start and end apart: 1 -> 2, of which waited for: 1 -> 2; matrix products, arithmetic and copies ran while one was open for 4% -> 4% of each run, Pallas kernels for 0% -> 0%
where the time goes in v1:
time: 193 us; the launch traced here: 192 us
  waiting for transfers between devices  70.7 us (37%)
  blocking collectives  61.6 us (32%)
  matrix products  25 us (13%)
  between operations  14.3 us (7%)
  other arithmetic  7.59 us (4%)
  local copies, waits for them, and re-layouts  6.81 us (4%)
  starting transfers between devices  5.93 us (3%)
    all_to_all x1, blocking collectives, per_device(): lax.all_to_all(buffer, 'dev', split_axis=0, concat_axis=0, tiled=True)  61.6 us
    all_to_all x1, waiting for transfers between devices, per_device(): lax.all_to_all(partial_out, 'dev', split_axis=0, concat_axis=0, tiled=True)  50.1 us
    all_gather x1, waiting for transfers between devices, per_device(): combined = jnp.sum(lax.all_gather(local_mix, 'side'), axis=0)  20.6 us
    all_to_all x1, starting transfers between devices, per_device(): lax.all_to_all(partial_out, 'dev', split_axis=0, concat_axis=0, tiled=True)  5.67 us
    dot_general x1, matrix products, per_device(): jnp.einsum('rec,ecd->rd', slot_gate, back.astype(jnp.float32), precision=...  5.22 us
    convert_element_type x1, local copies, waits for them, and re-layouts, per_device(): partial_out = jnp.einsum('scf,fd->scd', activation, w_down[0], preferred_...  4.27 us
  transfers between devices with their start and end apart: 2, of which 2 were waited for; matrix products, arithmetic and copies ran while one was open for 4% of the time, Pallas kernels for 0%

profile of v1, /device:TPU:2, one launch (start us, length us, event | category | flops | bytes accessed | tf_op | source)
XLA Modules:
  0.0 192.0 jit_solution(13323553420732560574)
XLA Ops:
  7.2 0.8 copy.38
  8.2 0.6 reduce-window.6
  9.4 0.7 reduce_sum.65
  10.1 0.7 broadcast_divide_fusion
  10.9 0.7 multiply_reduce_fusion
  11.7 0.7 convert_element_type.92
  12.4 1.1 fusion.32
  13.6 2.4 %convolution_convert_fusion = bf16[64,8,4096]{2,1,0:T(8,128)(2,1)S(1)} fusion(bf16[32,64,8]{0,2,1:T(8,128)(2,1)S(1)} %copy.43, bf16[32,4096]{1,0:T(8,128)(2,1)} %param.19, f32[4096]{0:T(1024)S(1)} %convert_element_type.92, f32[32]{0:T(128)S(1)} %add_rsqrt_fusion), kind=kOutput, calls=%fused_computation.7 | convolution fusion | flops 136839168 | bytes 4505728 | tf_op jit(solution)/shard_map/rec,rd->ecd/dot_general | solution.py:87
  16.0 61.6 %all_to_all.10 = bf16[64,8,4096]{2,1,0:T(8,128)(2,1)S(1)} all-to-all(bf16[64,8,4096]{2,1,0:T(8,128)(2,1)S(1)} %convolution_convert_fusion), channel_id=1, replica_groups=mesh['side'=2,'dev'=64] {'dev'}, dimensions={0} | all-to-all | bytes 8388608 | tf_op jit(solution)/shard_map/all_to_all | solution.py:90
  77.7 3.4 %fusion.4 = f32[64,8,768]{2,1,0:T(8,128)S(1)} fusion(bf16[64,8,4096]{2,1,0:T(8,128)(2,1)S(1)} %all_to_all.10, bf16[1,4096,768]{2,1,0:T(8,128)(2,1)S(1)} %bitcast.92), kind=kOutput, calls=%fused_computation.4 | convolution fusion | flops 3221225472 | bytes 12058624 | tf_op jit(solution)/shard_map/scd,df->scf/dot_general | solution.py:91
  81.2 3.5 %multiply_convert_fusion = bf16[64,8,768]{2,1,0:T(8,128)(2,1)S(1)} fusion(f32[64,8,768]{2,1,0:T(8,128)S(1)} %fusion.4, bf16[64,8,4096]{2,1,0:T(8,128)(2,1)S(1)} %all_to_all.10, bf16[1,4096,768]{2,1,0:T(8,128)(2,1)S(1)} %bitcast.94), kind=kOutput, calls=%fused_computation.15 | convolution fusion | flops 3223584768 | bytes 12845056 | tf_op jit(solution)/shard_map/scd,df->scf/dot_general | solution.py:92
  84.7 3.7 %fusion.6 = bf16[64,8,4096]{2,0,1:T(8,128)(2,1)S(1)} fusion(bf16[1,768,4096]{2,1,0:T(8,128)(2,1)S(1)} %bitcast.96, bf16[64,8,768]{2,1,0:T(8,128)(2,1)S(1)} %multiply_convert_fusion), kind=kOutput, calls=%fused_computation.6 | convolution fusion | flops 3223322624 | bytes 11272192 | tf_op jit(solution)/shard_map/scf,fd->scd/dot_general | solution.py:94
  88.4 4.3 %copy.45 = bf16[64,8,4096]{2,1,0:T(8,128)(2,1)} copy(bf16[64,8,4096]{2,0,1:T(8,128)(2,1)S(1)} %fusion.6) | data formatting | bytes 8388608 | tf_op jit(solution)/shard_map/convert_element_type | solution.py:96
  92.7 5.7 %all-to-all-start.1 = ((bf16[64,8,4096]{2,1,0:T(8,128)(2,1)}), bf16[64,8,4096]{2,1,0:T(8,128)(2,1)}, u32[]{:S(2)}, u32[]{:S(2)}) async-start(bf16[64,8,4096]{2,1,0:T(8,128)(2,1)} %copy.45), calls=%async_computation.1 | async-start | bytes 8388608 | tf_op jit(solution)/shard_map/all_to_all | solution.py:97
  98.4 0.3 all-gather.3.cloned.1.call-start
  99.0 0.2 fusion.49
  99.2 3.5 %fusion.48 = (f32[32,2,16]{2,1,0:T(2,128)S(1)}, f32[32,2,16,256]{3,2,1,0:T(8,128)S(1)}) fusion(bf16[32,2,16,128]{3,2,1,0:T(8,128)(2,1)S(1)} %bitcast.85, pred[32,256]{1,0:T(8,128)(4,1)S(1)} %iota_compare_fusion.4, bf16[32,256,256]{2,1,0:T(8,128)(2,1)} %param.14), kind=kOutput, calls=%fused_computation.59 | convolution fusion | flops 67894272 | bytes 5517312 | tf_op jit(solution)/shard_map/tgqd,tlgd->tgql/dot_general | solution.py:35
  102.8 50.1 %all-to-all-done.1 = bf16[64,8,4096]{2,1,0:T(8,128)(2,1)} async-done(((bf16[64,8,4096]{2,1,0:T(8,128)(2,1)}), bf16[64,8,4096]{2,1,0:T(8,128)(2,1)}, u32[]{:S(2)}, u32[]{:S(2)}) %all-to-all-start.1) | async-done | bytes 4194336 | tf_op jit(solution)/shard_map/all_to_all | solution.py:97
  152.9 5.2 %convolution_bitcast_fusion = f32[32,4096]{1,0:T(8,128)} fusion(f32[32,64,8]{0,2,1:T(8,128)S(1)} %copy.50, bf16[64,8,4096]{2,1,0:T(8,128)(2,1)} %all-to-all-done.1), kind=kOutput, calls=%fused_computation.8 | convolution fusion | flops 805306368 | bytes 4784128 | tf_op jit(solution)/shard_map/rec,ecd->rd/dot_general | solution.py:98
  158.2 0.4 fusion.30
  158.7 3.0 %fusion.26 = bf16[32,2,16,128]{3,2,1,0:T(8,128)(2,1)S(1)} fusion(f32[32,2,16,256]{3,2,1,0:T(8,128)S(1)} %get-tuple-element.7, f32[32,2,16]{2,1,0:T(2,128)S(1)} %get-tuple-element.5, f32[32,2,16]{2,1,0:T(2,128)S(1)} %multiply_maximum_fusion, f32[32,2,128]{2,1,0:T(2,128)S(1)} %reshape.127, f32[32,2,16]{2,1,0:T(2,128)S(1)} %get-tuple-element.4, ...), kind=kOutput, calls=%fused_computation.21 | convolution fusion | flops 68288512 | bytes 5550080 | tf_op jit(solution)/shard_map/tgql,tlgd->tgqd/dot_general | solution.py:51
  161.6 0.8 copy.80
  162.5 20.6 %all-gather.3.cloned.1.call-done = f32[64,4096]{1,0:T(8,128)} async-done(((f32[32,4096]{1,0:T(8,128)}), f32[64,4096]{1,0:T(8,128)}) %all-gather.3.cloned.1.call-update) | async-done | bytes 1048592 | tf_op jit(solution)/shard_map/all_gather | solution.py:101
  183.0 2.1 %reduce_sum.69 = bf16[32,4096]{1,0:T(8,128)(2,1)} reduce(f32[2,32,4096]{2,1,0:T(8,128)} %bitcast.83, f32[]{:T(128)} %constant.6.clone.1), dimensions={0}, to_apply=%region_9.10 | reduce | flops 131072 | bytes 1310724 | tf_op jit(solution)/shard_map/reduce_sum | solution.py:101
  (44 shorter events, 1.5 us)
Async XLA Ops:
  13.6 64.1 %slice-start = ((s8[6291456]{0:T(1024)(128)(4,1)}), s8[4194304]{0:T(1024)(128)(4,1)S(1)}, s32[]{:S(2)}) async-start(s8[6291456]{0:T(1024)(128)(4,1)} %bitcast.91), calls=%async_computation.3 | async-start | bytes 8388608
  16.0 61.7 %slice-start.1 = ((s8[6291456]{0:T(1024)(128)(4,1)}), s8[2097152]{0:T(1024)(128)(4,1)S(1)}, s32[]{:S(2)}) async-start(s8[6291456]{0:T(1024)(128)(4,1)} %bitcast.91), calls=%async_computation.4 | async-start | bytes 4194304
  16.0 65.1 %slice-start.2 = ((s8[6291456]{0:T(1024)(128)(4,1)}), s8[4194304]{0:T(1024)(128)(4,1)S(1)}, s32[]{:S(2)}) async-start(s8[6291456]{0:T(1024)(128)(4,1)} %bitcast.93), calls=%async_computation.5 | async-start | bytes 8388608
  77.6 3.5 %slice-start.3 = ((s8[6291456]{0:T(1024)(128)(4,1)}), s8[2097152]{0:T(1024)(128)(4,1)S(1)}, s32[]{:S(2)}) async-start(s8[6291456]{0:T(1024)(128)(4,1)} %bitcast.93), calls=%async_computation.6 | async-start | bytes 4194304
  77.6 7.1 %slice-start.4 = ((s8[6291456]{0:T(1024)(128)(4,1)}), s8[4194304]{0:T(1024)(128)(4,1)S(1)}, s32[]{:S(2)}) async-start(s8[6291456]{0:T(1024)(128)(4,1)} %bitcast.95), calls=%async_computation.7 | async-start | bytes 8388608
  81.1 3.6 %slice-start.5 = ((s8[6291456]{0:T(1024)(128)(4,1)}), s8[2097152]{0:T(1024)(128)(4,1)S(1)}, s32[]{:S(2)}) async-start(s8[6291456]{0:T(1024)(128)(4,1)} %bitcast.95), calls=%async_computation.8 | async-start | bytes 4194304
  92.7 6.0 %copy-start = (bf16[32,4096]{1,0:T(8,128)(2,1)S(1)}, bf16[32,4096]{1,0:T(8,128)(2,1)}, u32[]{:S(2)}) copy-start(bf16[32,4096]{1,0:T(8,128)(2,1)} %param.13) | copy-start | bytes 786436
  92.7 6.0 %copy-start.1 = (bf16[32,256]{1,0:T(8,128)(2,1)S(1)}, bf16[32,256]{1,0:T(8,128)(2,1)}, u32[]{:S(2)}) copy-start(bf16[32,256]{1,0:T(8,128)(2,1)} %param.16) | copy-start | bytes 49156
  92.7 6.0 %copy-start.2 = (bf16[32,256]{1,0:T(8,128)(2,1)S(1)}, bf16[32,256]{1,0:T(8,128)(2,1)}, u32[]{:S(2)}) copy-start(bf16[32,256]{1,0:T(8,128)(2,1)} %param.17) | copy-start | bytes 49156
  92.7 6.2 %copy-start.3 = (s32[32]{0:T(128)S(1)}, s32[32]{0:T(128)}, u32[]{:S(2)}) copy-start(s32[32]{0:T(128)} %param.18) | copy-start | bytes 388
  92.7 60.2 %all-to-all-start.1 = ((bf16[64,8,4096]{2,1,0:T(8,128)(2,1)}), bf16[64,8,4096]{2,1,0:T(8,128)(2,1)}, u32[]{:S(2)}, u32[]{:S(2)}) async-start(bf16[64,8,4096]{2,1,0:T(8,128)(2,1)} %copy.45), calls=%async_computation.1 | async-start | bytes 8388608 | tf_op jit(solution)/shard_map/all_to_all | solution.py:97
  98.4 84.7 %all-gather.3.cloned.1.call-start = ((), (), s32[]{:S(2)}) async-start(), calls=%async_computation.2 | async-start | bytes 1572864 | tf_op jit(solution)/shard_map/all_gather | solution.py:101
Sparse Core Ops, SparseCore 0:
  158.2 24.7 all-gather.2
